TPU v7x, 32 devices: a whole 2x2x4 slice. The times are simulated.
32 devices in a mesh: grp: 8 (over z, y), tp: 2 (over core), fs: 2 (over x).
Axes of the slice: x: 2, y: 2, z: 4, core: 2. Of those that a mesh axis runs over, the one named last changes fastest.
Arguments:
- tokens: bfloat16 [512, 4, 8192], P('grp', None, ('tp', 'fs')), may hold values from -64 to 64
- norm_gain: bfloat16 [8192], P(('tp', 'fs')), may hold values from 0.25 to 1.75
- queries: bfloat16 [512, 4, 8192], P('grp', None, ('tp', 'fs')), may hold values from -64 to 64
- rotated_key_cache: bfloat16 [512, 32, 1024], P('grp', None, ('tp', 'fs')), may hold values from -6 to 6
- head_value_cache: bfloat16 [512, 32, 1024], P('grp', None, ('tp', 'fs')), may hold values from -6 to 6
- lengths: int32 [512], P('grp'), may hold values from 2 to 32
- master: float32 [8192, 2048], P('grp', ('tp', 'fs')), may hold values from -0.0625 to 0.0625
- moment_first: float32 [8192, 2048], P('grp', ('tp', 'fs')), may hold values from -4 to 4
- moment_second: float32 [8192, 2048], P('grp', ('tp', 'fs')), may hold values from 0.1 to 1
- gradient: float32 [8192, 2048], P('grp', ('tp', 'fs')), may hold values from -6 to 6
Outputs:
- attended: bfloat16 [512, 4, 8192], P('grp', None, ('tp', 'fs'))
- appended: bfloat16 [512, 4, 2048], P('grp', None, ('tp', 'fs'))
- new_master: float32 [8192, 2048], P('grp', ('tp', 'fs'))
- new_first: float32 [8192, 2048], P('grp', ('tp', 'fs'))
- new_second: float32 [8192, 2048], P('grp', ('tp', 'fs'))
All inputs are finite; a program needn't handle non-finite values.
Results may differ from a plain program's by a relative error of at most 0.0057.
Values may be sent and summed in bfloat16 or wider, within the bound.
A program may use at most 128 MiB of HBM per device.

v0:
```python
import jax
import jax.numpy as jnp
from jax import lax
from jax.sharding import PartitionSpec as P

MODEL_WIDTH = 8192
QUERY_HEADS = 64
KEY_VALUE_HEADS = 8
HEAD_SIZE = 128
beta_first = 0.9
beta_second = 0.999
correct_first = 0.9999734386011124
correct_second = 0.09520785288629038
adam_eps = 1e-08
learn_rate = 0.003
decay_rate = 0.1
norm_eps = 1e-06
rope_base = 1000000.0


def rotate(keys, positions):
    halfway = keys.shape[-1] // 2
    frequency = rope_base ** (-(jnp.arange(halfway, dtype=jnp.float32) * 2.0 / keys.shape[-1]))
    angles = positions[:, :, None] * frequency[None, None, :]
    cosine = jnp.cos(angles)[:, :, None, :]
    sine = jnp.sin(angles)[:, :, None, :]
    first_half = keys[..., :halfway]
    second_half = keys[..., halfway:]
    return jnp.concatenate(
        [first_half * cosine - second_half * sine, second_half * cosine + first_half * sine],
        axis=-1,
    )


def attention(queries, rotated_key_cache, head_value_cache, key_new, value_new, lengths):
    batch_rows, steps = (queries.shape[0], queries.shape[1])
    window = rotated_key_cache.shape[1]
    kv_heads = rotated_key_cache.shape[2] // HEAD_SIZE
    sharing_factor = QUERY_HEADS // KEY_VALUE_HEADS
    factor = HEAD_SIZE ** (-0.5)
    query_heads = queries.reshape(batch_rows, steps, kv_heads, sharing_factor, HEAD_SIZE)
    cache_key_seeds = rotated_key_cache.reshape(batch_rows, window, kv_heads, HEAD_SIZE)
    cache_values = head_value_cache.reshape(batch_rows, window, kv_heads, HEAD_SIZE)
    scores_cached = (
        jnp.einsum(
            "rsxgd,rlxd->rxgsl", query_heads, cache_key_seeds, preferred_element_type=jnp.float32
        )
        * factor
    )
    scores_fresh = (
        jnp.einsum("rsxgd,ruxd->rxgsu", query_heads, key_new, preferred_element_type=jnp.float32)
        * factor
    )
    present = (jnp.arange(window, dtype=jnp.int32)[None, :] < lengths[:, None])[
        :, None, None, None, :
    ]
    causal = (
        jnp.arange(steps, dtype=jnp.int32)[None, :] <= jnp.arange(steps, dtype=jnp.int32)[:, None]
    )[None, None, None, :, :]
    scores_cached = jnp.where(present, scores_cached, -jnp.inf)
    scores_fresh = jnp.where(causal, scores_fresh, -jnp.inf)
    ceiling = jnp.maximum(
        jnp.max(scores_cached, axis=-1, keepdims=True),
        jnp.max(scores_fresh, axis=-1, keepdims=True),
    )
    probs_cached = jnp.exp(scores_cached - ceiling)
    probs_fresh = jnp.exp(scores_fresh - ceiling)
    denom = jnp.sum(probs_cached, axis=-1, keepdims=True) + jnp.sum(
        probs_fresh, axis=-1, keepdims=True
    )
    weights_cached = probs_cached.astype(jnp.bfloat16)
    weights_fresh = probs_fresh.astype(jnp.bfloat16)
    blended = jnp.einsum(
        "rxgsl,rlxd->rsxgd", weights_cached, cache_values, preferred_element_type=jnp.float32
    )
    blended = blended + jnp.einsum(
        "rxgsu,ruxd->rsxgd", weights_fresh, value_new, preferred_element_type=jnp.float32
    )
    blended = blended / jnp.transpose(denom, (0, 3, 1, 2, 4))
    return blended.astype(jnp.bfloat16).reshape(
        batch_rows, steps, kv_heads * sharing_factor * HEAD_SIZE
    )


def shards(
    tokens,
    norm_gain,
    queries,
    rotated_key_cache,
    head_value_cache,
    lengths,
    master,
    moment_first,
    moment_second,
    gradient,
):
    average = beta_first * moment_first + (1.0 - beta_first) * gradient
    variance = beta_second * moment_second + (1.0 - beta_second) * gradient * gradient
    update = average / correct_first / (jnp.sqrt(variance / correct_second) + adam_eps)
    renewed = master - learn_rate * (update + decay_rate * master)
    layer_half = renewed.astype(jnp.bfloat16)
    widened, gain_whole = (
        lax.all_gather(tokens, ("tp", "fs"), axis=2, tiled=True),
        lax.all_gather(norm_gain, ("tp", "fs"), axis=0, tiled=True),
    )
    mean_square = (
        jnp.einsum("rsd,rsd->rs", widened, widened, preferred_element_type=jnp.float32)[..., None]
        / MODEL_WIDTH
    )
    normed = (widened * lax.rsqrt(mean_square + norm_eps) * gain_whole.astype(jnp.float32)).astype(
        jnp.bfloat16
    )
    batch_rows, steps = (tokens.shape[0], tokens.shape[1])
    flattened = normed.reshape(batch_rows * steps, MODEL_WIDTH)
    columns = layer_half.shape[1]
    gathered = lax.all_gather(layer_half, "grp", axis=0, tiled=True)
    projected_output = jnp.dot(flattened, gathered, preferred_element_type=jnp.float32)
    kv_heads = columns // (2 * HEAD_SIZE)
    projected_output = projected_output.reshape(batch_rows, steps, kv_heads, 2, HEAD_SIZE)
    positions = (lengths[:, None] + jnp.arange(steps, dtype=jnp.int32)[None, :]).astype(jnp.float32)
    key_new = rotate(projected_output[:, :, :, 0, :], positions).astype(jnp.bfloat16)
    value_new = projected_output[:, :, :, 1, :].astype(jnp.bfloat16)
    appended = jnp.stack([key_new, value_new], axis=3).reshape(batch_rows, steps, columns)
    attended = attention(queries, rotated_key_cache, head_value_cache, key_new, value_new, lengths)
    return (attended, appended, renewed, average, variance)


def solution(mesh):
    in_specs = (
        P("grp", None, ("tp", "fs")),
        P(("tp", "fs")),
        P("grp", None, ("tp", "fs")),
        P("grp", None, ("tp", "fs")),
        P("grp", None, ("tp", "fs")),
        P("grp"),
        P("grp", ("tp", "fs")),
        P("grp", ("tp", "fs")),
        P("grp", ("tp", "fs")),
        P("grp", ("tp", "fs")),
    )
    out_specs = (
        P("grp", None, ("tp", "fs")),
        P("grp", None, ("tp", "fs")),
        P("grp", ("tp", "fs")),
        P("grp", ("tp", "fs")),
        P("grp", ("tp", "fs")),
    )
    return jax.shard_map(shards, mesh=mesh, in_specs=in_specs, out_specs=out_specs, check_vma=False)
```

profile of v0, /device:TPU:0, one launch (start us, length us, event | category | flops | bytes accessed | tf_op | source)
XLA Modules:
  0.0 219.5 jit_solution(13725057092368029306)
XLA Ops:
  7.2 0.7 all-gather.3.cloned.1.call-update
  8.0 7.8 %fusion.33 = (bf16[1024,512]{1,0:T(8,128)(2,1)}, f32[1024,512]{1,0:T(8,128)}, f32[1024,512]{1,0:T(8,128)}, f32[1024,512]{1,0:T(8,128)}) fusion(f32[1024,512]{1,0:T(8,128)} %param.16, f32[1024,512]{1,0:T(8,128)} %param.19, f32[1024,512]{1,0:T(8,128)} %param.17, f32[1024,512]{1,0:T(8,128)} %param.18), kind=kLoop, calls=%fused_computation.56 | loop fusion | flops 8388608 | bytes 15728640 | tf_op jit(solution)/shard_map/convert_element_type | solution.py:101
  15.8 10.8 %all_gather.10 = bf16[8192]{0:T(1024)(128)(2,1)S(1)} all-gather(bf16[2048]{0:T(1024)(128)(2,1)S(1)} %copy-done.6), channel_id=1, replica_groups=mesh['grp'=8,'tp'=2,'fs'=2] {'tp','fs'}, dimensions={0}, use_global_device_ids=true | all-gather | bytes 20480 | tf_op jit(solution)/shard_map/all_gather | solution.py:104
  26.7 1.5 reshape.145
  28.2 1.1 reshape.144
  29.3 1.1 reshape.146
  30.5 0.5 multiply_cosine_fusion
  31.0 2.4 %bitcast_reduce_fusion = (f32[64,2,8,4]{2,3,1,0:T(4,128)S(1)}, f32[64,2,32,4,8]{2,4,3,1,0:T(8,128)S(1)}) fusion(pred[64,32]{1,0:T(8,128)(4,1)S(1)} %iota_compare_fusion, bf16[64,4,2,8,128]{4,3,2,1,0:T(8,128)(2,1)} %reshape.145, bf16[64,32,2,128,1]{3,2,1,0,4:T(2,128)(2,1)} %bitcast.58), kind=kOutput, calls=%fused_computation.14 | convolution fusion | flops 33943552 | bytes 2639872 | tf_op jit(solution)/shard_map/rsxgd,rlxd->rxgsl/dot_general | solution.py:45
  33.4 13.5 %all-gather.3.cloned.1.call-done = bf16[64,4,8192]{2,1,0:T(4,128)(2,1)} async-done(((bf16[64,4,2048]{2,1,0:T(4,128)(2,1)}), bf16[64,4,8192]{2,1,0:T(4,128)(2,1)}) %all-gather.3.cloned.1.call-update) | async-done | bytes 4194320 | tf_op jit(solution)/shard_map/all_gather | solution.py:103
  46.9 4.6 %fusion.2 = f32[64,4]{1,0:T(8,128)S(1)} fusion(bf16[64,4,8192]{2,1,0:T(4,128)(2,1)} %all-gather.3.cloned.1.call-done), kind=kLoop, calls=%fused_computation.4 | loop fusion | flops 6291200 | bytes 4195328 | tf_op jit(solution)/shard_map/rsd,rsd->rs/dot_general | solution.py:107
  51.5 4.7 %fusion.3 = bf16[64,4,8192,1,1]{2,1,0,4,3:T(4,128)(2,1)} fusion(bf16[64,4,8192]{2,1,0:T(4,128)(2,1)S(1)} %copy-done, f32[8192]{0:T(1024)S(1)} %convert_element_type.44, f32[64,4]{1,0:T(8,128)S(1)} %add_rsqrt_fusion), kind=kLoop, calls=%fused_computation.5 | loop fusion | flops 8388608 | bytes 8422400 | tf_op jit(solution)/shard_map/convert_element_type | solution.py:110
  56.3 117.3 %all-gather.5.cloned.1.call-done = bf16[8192,512]{1,0:T(8,128)(2,1)} async-done(((bf16[1024,512]{1,0:T(8,128)(2,1)}), bf16[8192,512]{1,0:T(8,128)(2,1)}) %all-gather.5.cloned.1.call-update) | async-done | bytes 8388624 | tf_op jit(solution)/shard_map/all_gather | solution.py:116
  173.6 11.9 %copy.41 = bf16[512,8192]{1,0:T(8,128)(2,1)} copy(bf16[512,8192]{0,1:T(8,128)(2,1)} %bitcast.53) | data formatting | bytes 16777216 | tf_op jit(solution)/shard_map/dot_general | solution.py:117
  185.5 13.5 %fusion.4 = f32[64,4,2,2,128]{4,0,3,2,1:T(8,128)S(1)} fusion(bf16[2,2,128,8192,1]{3,2,1,0,4:T(8,128)(2,1)} %bitcast.54, bf16[64,4,8192,1,1]{2,1,0,4,3:T(4,128)(2,1)} %fusion.3), kind=kOutput, calls=%fused_computation.6 | convolution fusion | flops 2147483648 | bytes 13107200 | tf_op jit(solution)/shard_map/dot_general | solution.py:117
  199.4 0.9 copy-done.5
  200.3 4.7 %fusion.35 = (f32[64,2,8,4]{2,3,1,0:T(4,128)S(1)}, f32[64,2,8,4,4]{2,4,3,1,0:T(4,128)S(1)}) fusion(bf16[64,4,2,8,128]{4,3,2,1,0:T(8,128)(2,1)S(1)} %copy-done.5, bf16[64,4,2,128,1]{3,0,2,1,4:T(8,128)(2,1)S(1)} %maximum_bitcast_fusion, pred[4,4]{1,0:T(4,128)(4,1)S(1)} %iota_compare_fusion.1), kind=kOutput, calls=%fused_computation.57 | convolution fusion | flops 4239360 | bytes 1261584 | tf_op jit(solution)/shard_map/rsxgd,ruxd->rxgsu/dot_general | solution.py:51
  205.1 1.0 fusion.25
  206.0 1.4 fusion.10
  207.5 1.4 fusion.14
  208.9 1.2 fusion.8
  210.1 0.2 copy.72
  210.3 1.1 reshape.157
  211.6 0.3 copy.73
  211.8 0.8 reshape.158
  (32 shorter events, 0.8 us)
Async XLA Ops:
  7.2 39.8 %all-gather.3.cloned.1.call-start = ((), (), s32[]{:S(2)}) async-start(), calls=%async_computation | async-start | bytes 5242880 | tf_op jit(solution)/shard_map/all_gather | solution.py:103
  7.9 7.9 %copy-start.6 = (bf16[2048]{0:T(1024)(128)(2,1)S(1)}, bf16[2048]{0:T(1024)(128)(2,1)}, u32[]{:S(2)}) copy-start(bf16[2048]{0:T(1024)(128)(2,1)} %param.11) | copy-start | bytes 12292
  7.9 18.8 %copy-start.1 = (bf16[64,4,2048]{2,1,0:T(4,128)(2,1)S(1)}, bf16[64,4,2048]{2,1,0:T(4,128)(2,1)}, u32[]{:S(2)}) copy-start(bf16[64,4,2048]{2,1,0:T(4,128)(2,1)} %param.12) | copy-start | bytes 3145732
  7.9 165.7 %all-gather.5.cloned.1.call-start = ((), (), s32[]{:S(2)}) async-start(), calls=%async_computation.1 | async-start | bytes 9437184 | tf_op jit(solution)/shard_map/all_gather | solution.py:116
  15.8 12.4 %copy-start.2 = (bf16[64,32,256]{2,1,0:T(8,128)(2,1)S(1)}, bf16[64,32,256]{2,1,0:T(8,128)(2,1)}, u32[]{:S(2)}) copy-start(bf16[64,32,256]{2,1,0:T(8,128)(2,1)} %param.13) | copy-start | bytes 3145732
  26.7 2.6 %copy-start.3 = (bf16[64,32,256]{2,1,0:T(8,128)(2,1)S(1)}, bf16[64,32,256]{2,1,0:T(8,128)(2,1)}, u32[]{:S(2)}) copy-start(bf16[64,32,256]{2,1,0:T(8,128)(2,1)} %param.14) | copy-start | bytes 3145732
  28.2 2.2 %copy-start.7 = (s32[64]{0:T(128)S(1)}, s32[64]{0:T(128)}, u32[]{:S(2)}) copy-start(s32[64]{0:T(128)} %param.15) | copy-start | bytes 772
  46.9 4.6 %copy-start = (bf16[64,4,8192]{2,1,0:T(4,128)(2,1)S(1)}, bf16[64,4,8192]{2,1,0:T(4,128)(2,1)}, u32[]{:S(2)}) copy-start(bf16[64,4,8192]{2,1,0:T(4,128)(2,1)} %all-gather.3.cloned.1.call-done) | copy-start | bytes 12582916
  199.0 1.2 copy-start.5
  205.1 2.4 %copy-start.4 = (bf16[64,32,2,128]{3,2,1,0:T(2,128)(2,1)S(1)}, bf16[64,32,2,128]{3,2,1,0:T(2,128)(2,1)}, u32[]{:S(2)}) copy-start(bf16[64,32,2,128]{3,2,1,0:T(2,128)(2,1)} %reshape.146) | copy-start | bytes 3145732
Sparse Core Ops, SparseCore 0:
  9.5 37.3 all-gather.2
  49.0 124.5 all-gather.4
where the time goes:
time: 220 us; the launch traced here: 219 us
  waiting for transfers between devices  132 us (60%)
  matrix products  23.2 us (11%)
  other arithmetic  20.7 us (9%)
  local copies, waits for them, and re-layouts  18.9 us (9%)
  between operations  14.2 us (6%)
  blocking collectives  10.8 us (5%)
    all_gather x1, waiting for transfers between devices, shards(): gathered = lax.all_gather(layer_half, 'grp', axis=0, tiled=True)  117 us
    dot_general x1, matrix products, shards(): jnp.dot(flattened, gathered, preferred_element_type=jnp.float32)  13.5 us
    all_gather x1, waiting for transfers between devices, shards(): lax.all_gather(tokens, ('tp', 'fs'), axis=2, tiled=True)  13.5 us
    dot_general x1, local copies, waits for them, and re-layouts, shards(): jnp.dot(flattened, gathered, preferred_element_type=jnp.float32)  11.9 us
    all_gather x1, blocking collectives, shards(): lax.all_gather(norm_gain, ('tp', 'fs'), axis=0, tiled=True)  10.8 us
    convert_element_type x1, other arithmetic, shards(): layer_half = renewed.astype(jnp.bfloat16)  7.82 us
    dot_general x1, matrix products, attention(): jnp.einsum('rsxgd,ruxd->rxgsu', query_heads, key_new, preferred_element_t...  4.73 us
    convert_element_type x1, other arithmetic, shards(): (widened * lax.rsqrt(mean_square + norm_eps) * gain_whole.astype(jnp.floa...  4.72 us
  transfers between devices with their start and end apart: 2, of which 2 were waited for; matrix products, arithmetic and copies ran while one was open for 11% of the time, Pallas kernels for 0%

commit v1 on v0

--- a/solution.py
+++ b/solution.py
@@ -16,6 +16,12 @@
 decay_rate = 0.1
 norm_eps = 1e-06
 rope_base = 1000000.0
+
+
+def gathered_along(x, axis, dim):
+    pieces = lax.all_gather(x, axis, axis=0, tiled=False)
+    result = jnp.concatenate(pieces, axis=dim)
+    return result
 
 
 def rotate(keys, positions):
@@ -100,7 +106,7 @@
     renewed = master - learn_rate * (update + decay_rate * master)
     layer_half = renewed.astype(jnp.bfloat16)
     widened, gain_whole = (
-        lax.all_gather(tokens, ("tp", "fs"), axis=2, tiled=True),
+        gathered_along(tokens, ("tp", "fs"), 2),
         lax.all_gather(norm_gain, ("tp", "fs"), axis=0, tiled=True),
     )
     mean_square = (

time: 220 us -> 213 us (0.968)
  waiting for transfers between devices: 132 us -> 104 us
  local copies, waits for them, and re-layouts: 18.9 us -> 42.3 us
  matrix products: 23.2 us -> 15.9 us
  other arithmetic: 20.7 us -> 24.4 us
    all_gather x1, waiting for transfers between devices: 117 us -> 90.3 us  [shards(): gathered = lax.all_gather(layer_half, 'grp', axis=0, tiled=True)]
    reshape x0 -> x1, local copies, waits for them, and re-layouts: none -> 7.92 us  [gathered_along(): result = jnp.concatenate(pieces, axis=dim)]
    convert_element_type x0 -> x1, local copies, waits for them, and re-layouts: none -> 7.75 us  [shards(): (widened * lax.rsqrt(mean_square + norm_eps) * gain_whole.astype(jnp.floa...]
    all_gather x0 -> x1, local copies, waits for them, and re-layouts: none -> 7.45 us  [gathered_along(): pieces = lax.all_gather(x, axis, axis=0, tiled=False)]
    dot_general x1, matrix products: 13.5 us -> 6.28 us  [shards(): jnp.dot(flattened, gathered, preferred_element_type=jnp.float32)]
    convert_element_type x1, other arithmetic: 4.72 us -> 9.77 us  [shards(): (widened * lax.rsqrt(mean_square + norm_eps) * gain_whole.astype(jnp.floa...]
  transfers between devices with their start and end apart: 2 -> 2, of which waited for: 2 -> 2; matrix products, arithmetic and copies ran while one was open for 11% -> 24% of each run, Pallas kernels for 0% -> 0%
where the time goes in v1:
time: 213 us; the launch traced here: 212 us
  waiting for transfers between devices  104 us (49%)
  local copies, waits for them, and re-layouts  42.3 us (20%)
  other arithmetic  24.4 us (11%)
  matrix products  15.9 us (7%)
  between operations  14.2 us (7%)
  blocking collectives  11.1 us (5%)
    all_gather x1, waiting for transfers between devices, shards(): gathered = lax.all_gather(layer_half, 'grp', axis=0, tiled=True)  90.3 us
    all_gather x1, waiting for transfers between devices, gathered_along(): pieces = lax.all_gather(x, axis, axis=0, tiled=False)  13.2 us
    dot_general x1, local copies, waits for them, and re-layouts, shards(): jnp.dot(flattened, gathered, preferred_element_type=jnp.float32)  11.9 us
    all_gather x1, blocking collectives, shards(): lax.all_gather(norm_gain, ('tp', 'fs'), axis=0, tiled=True)  11.1 us
    convert_element_type x1, other arithmetic, shards(): (widened * lax.rsqrt(mean_square + norm_eps) * gain_whole.astype(jnp.floa...  9.77 us
    reshape x1, local copies, waits for them, and re-layouts, gathered_along(): result = jnp.concatenate(pieces, axis=dim)  7.92 us
    convert_element_type x1, other arithmetic, shards(): layer_half = renewed.astype(jnp.bfloat16)  7.79 us
    convert_element_type x1, local copies, waits for them, and re-layouts, shards(): (widened * lax.rsqrt(mean_square + norm_eps) * gain_whole.astype(jnp.floa...  7.75 us
  transfers between devices with their start and end apart: 2, of which 2 were waited for; matrix products, arithmetic and copies ran while one was open for 24% of the time, Pallas kernels for 0%

profile of v1, /device:TPU:0, one launch (start us, length us, event | category | flops | bytes accessed | tf_op | source)
XLA Modules:
  0.0 212.2 jit_solution(2906579438122613036)
XLA Ops:
  7.2 0.7 all-gather.6.cloned.1.call-update
  8.0 7.8 %fusion.30 = (bf16[1024,512]{1,0:T(8,128)(2,1)}, f32[1024,512]{1,0:T(8,128)}, f32[1024,512]{1,0:T(8,128)}, f32[1024,512]{1,0:T(8,128)}) fusion(f32[1024,512]{1,0:T(8,128)} %param.16, f32[1024,512]{1,0:T(8,128)} %param.19, f32[1024,512]{1,0:T(8,128)} %param.17, f32[1024,512]{1,0:T(8,128)} %param.18), kind=kLoop, calls=%fused_computation.54 | loop fusion | flops 8388608 | bytes 15728640 | tf_op jit(solution)/shard_map/convert_element_type | solution.py:107
  15.8 11.1 %all_gather.14 = bf16[8192]{0:T(1024)(128)(2,1)S(1)} all-gather(bf16[2048]{0:T(1024)(128)(2,1)S(1)} %copy-done.6), channel_id=1, replica_groups=mesh['grp'=8,'tp'=2,'fs'=2] {'tp','fs'}, dimensions={0}, use_global_device_ids=true | all-gather | bytes 20480 | tf_op jit(solution)/shard_map/all_gather | solution.py:110
  26.9 1.5 reshape.175
  28.4 1.2 reshape.174
  29.6 1.1 reshape.178
  31.3 2.4 %bitcast_reduce_fusion = (f32[64,2,8,4]{2,3,1,0:T(4,128)S(1)}, f32[64,2,32,4,8]{2,4,3,1,0:T(8,128)S(1)}) fusion(pred[64,32]{1,0:T(8,128)(4,1)S(1)} %iota_compare_fusion, bf16[64,4,2,8,128]{4,3,2,1,0:T(8,128)(2,1)} %reshape.175, bf16[64,32,2,128,1]{3,2,1,0,4:T(2,128)(2,1)} %bitcast.72), kind=kOutput, calls=%fused_computation.12 | convolution fusion | flops 33943552 | bytes 2639872 | tf_op jit(solution)/shard_map/rsxgd,rlxd->rxgsl/dot_general | solution.py:51
  33.7 13.2 %all-gather.6.cloned.1.call-done = bf16[256,4,2048]{2,1,0:T(4,128)(2,1)} async-done(((bf16[64,4,2048]{2,1,0:T(4,128)(2,1)}), bf16[256,4,2048]{2,1,0:T(4,128)(2,1)}) %all-gather.6.cloned.1.call-update) | async-done | bytes 4194320 | tf_op jit(solution)/shard_map/all_gather | solution.py:22
  46.9 7.5 %copy.98 = bf16[4,64,4,2048]{3,0,1,2:T(4,128)(2,1)} copy(bf16[4,64,4,2048]{3,2,1,0:T(4,128)(2,1)} %bitcast.64) | data formatting | bytes 8388608 | tf_op jit(solution)/shard_map/all_gather | solution.py:22
  54.4 7.9 %reshape.177 = bf16[64,4,8192]{2,0,1:T(8,128)(2,1)} reshape(bf16[64,4,4,2048]{3,2,0,1:T(4,128)(2,1)} %bitcast.66) | data formatting | bytes 8388608 | tf_op jit(solution)/shard_map/reshape | solution.py:23
  62.3 3.3 %fusion = f32[64,4]{0,1:T(4,128)S(1)} fusion(bf16[64,4,8192]{2,0,1:T(8,128)(2,1)} %reshape.177), kind=kLoop, calls=%fused_computation.1 | loop fusion | flops 6291200 | bytes 4195328 | tf_op jit(solution)/shard_map/rsd,rsd->rs/dot_general | solution.py:113
  65.8 9.8 %multiply_convert_fusion = bf16[64,4,4,2048]{3,2,0,1:T(4,128)(2,1)} fusion(f32[4,2048]{1,0:T(4,128)S(1)} %reshape.181, f32[64,4]{0,1:T(4,128)S(1)} %add_rsqrt_fusion, bf16[4,64,4,2048]{3,2,1,0:T(4,128)(2,1)S(1)} %bitcast.65), kind=kLoop, calls=%fused_computation.2 | loop fusion | flops 8388608 | bytes 8422400 | tf_op jit(solution)/shard_map/convert_element_type | solution.py:116
  75.5 7.7 %reshape.186 = bf16[64,4,8192,1,1]{2,0,1,3,4:T(8,128)(2,1)} reshape(bf16[64,4,4,2048]{3,2,0,1:T(4,128)(2,1)} %multiply_convert_fusion) | data formatting | bytes 8388608 | tf_op jit(solution)/shard_map/convert_element_type | solution.py:116
  83.3 90.3 %all-gather.4.cloned.1.call-done = bf16[8192,512]{1,0:T(8,128)(2,1)} async-done(((bf16[1024,512]{1,0:T(8,128)(2,1)}), bf16[8192,512]{1,0:T(8,128)(2,1)}) %all-gather.4.cloned.1.call-update) | async-done | bytes 8388624 | tf_op jit(solution)/shard_map/all_gather | solution.py:122
  173.6 11.9 %copy.42 = bf16[512,8192]{1,0:T(8,128)(2,1)} copy(bf16[512,8192]{0,1:T(8,128)(2,1)} %bitcast.67) | data formatting | bytes 16777216 | tf_op jit(solution)/shard_map/dot_general | solution.py:123
  185.5 6.3 %fusion.1 = f32[64,4,2,2,128]{4,0,3,2,1:T(8,128)S(1)} fusion(bf16[2,2,128,8192,1]{3,2,1,0,4:T(8,128)(2,1)} %bitcast.68, bf16[64,4,8192,1,1]{2,0,1,3,4:T(8,128)(2,1)} %reshape.186), kind=kOutput, calls=%fused_computation.3 | convolution fusion | flops 2147483648 | bytes 13107200 | tf_op jit(solution)/shard_map/dot_general | solution.py:123
  192.1 0.9 copy-done.5
  193.0 4.7 %fusion.32 = (f32[64,2,8,4]{2,3,1,0:T(4,128)S(1)}, f32[64,2,8,4,4]{2,4,3,1,0:T(4,128)S(1)}) fusion(bf16[64,4,2,8,128]{4,3,2,1,0:T(8,128)(2,1)S(1)} %copy-done.5, bf16[64,4,2,128,1]{3,0,2,1,4:T(8,128)(2,1)S(1)} %maximum_bitcast_fusion, pred[4,4]{1,0:T(4,128)(4,1)S(1)} %iota_compare_fusion.1), kind=kOutput, calls=%fused_computation.55 | convolution fusion | flops 4239360 | bytes 1261584 | tf_op jit(solution)/shard_map/rsxgd,ruxd->rxgsu/dot_general | solution.py:57
  197.8 1.0 fusion.22
  198.8 1.4 fusion.7
  200.2 1.4 fusion.11
  201.7 1.2 fusion.5
  203.1 1.1 reshape.192
  204.6 0.8 reshape.193
  (35 shorter events, 2.0 us)
Async XLA Ops:
  7.2 39.8 %all-gather.6.cloned.1.call-start = ((), (), s32[]{:S(2)}) async-start(), calls=%async_computation.1 | async-start | bytes 5242880 | tf_op jit(solution)/shard_map/all_gather | solution.py:22
  7.9 7.9 %copy-start.6 = (bf16[2048]{0:T(1024)(128)(2,1)S(1)}, bf16[2048]{0:T(1024)(128)(2,1)}, u32[]{:S(2)}) copy-start(bf16[2048]{0:T(1024)(128)(2,1)} %param.11) | copy-start | bytes 12292
  7.9 19.0 %copy-start.1 = (bf16[64,4,2048]{2,1,0:T(4,128)(2,1)S(1)}, bf16[64,4,2048]{2,1,0:T(4,128)(2,1)}, u32[]{:S(2)}) copy-start(bf16[64,4,2048]{2,1,0:T(4,128)(2,1)} %param.12) | copy-start | bytes 3145732
  7.9 165.7 %all-gather.4.cloned.1.call-start = ((), (), s32[]{:S(2)}) async-start(), calls=%async_computation | async-start | bytes 9437184 | tf_op jit(solution)/shard_map/all_gather | solution.py:122
  15.8 12.6 %copy-start.2 = (bf16[64,32,256]{2,1,0:T(8,128)(2,1)S(1)}, bf16[64,32,256]{2,1,0:T(8,128)(2,1)}, u32[]{:S(2)}) copy-start(bf16[64,32,256]{2,1,0:T(8,128)(2,1)} %param.13) | copy-start | bytes 3145732
  26.9 2.7 %copy-start.3 = (bf16[64,32,256]{2,1,0:T(8,128)(2,1)S(1)}, bf16[64,32,256]{2,1,0:T(8,128)(2,1)}, u32[]{:S(2)}) copy-start(bf16[64,32,256]{2,1,0:T(8,128)(2,1)} %param.14) | copy-start | bytes 3145732
  28.4 2.3 %copy-start.7 = (s32[64]{0:T(128)S(1)}, s32[64]{0:T(128)}, u32[]{:S(2)}) copy-start(s32[64]{0:T(128)} %param.15) | copy-start | bytes 772
  62.3 3.5 %copy-start = (bf16[256,4,2048]{2,1,0:T(4,128)(2,1)S(1)}, bf16[256,4,2048]{2,1,0:T(4,128)(2,1)}, u32[]{:S(2)}) copy-start(bf16[256,4,2048]{2,1,0:T(4,128)(2,1)} %all-gather.6.cloned.1.call-done) | copy-start | bytes 12582916
  191.8 1.2 copy-start.5
  197.8 2.4 %copy-start.4 = (bf16[64,32,2,128]{3,2,1,0:T(2,128)(2,1)S(1)}, bf16[64,32,2,128]{3,2,1,0:T(2,128)(2,1)}, u32[]{:S(2)}) copy-start(bf16[64,32,2,128]{3,2,1,0:T(2,128)(2,1)} %reshape.178) | copy-start | bytes 3145732
Sparse Core Ops, SparseCore 0:
  9.5 37.3 all-gather.5
  49.0 124.5 all-gather.3
